TPU v7x, 128 devices: a whole 4x4x4 slice. The times are simulated.
128 devices in a mesh: ep: 64 (over z, y, x_hi, core), dp: 2 (over x_lo).
Axes of the slice: x: 4 (x_hi: 2, x_lo: 2; x = x_hi * 2 + x_lo), y: 4, z: 4, core: 2. Of those that a mesh axis runs over, the one named last changes fastest.
Arguments:
- hidden: bfloat16 [3, 2048, 4096], P(None, ('dp', 'ep')), parts along dimension 1, may hold values from -6 to 6
- expert_ids: int32 [3, 2048, 8], P(None, ('dp', 'ep')), parts along dimension 1, may hold values from 0 to 63, all different within a row; in each aligned block of 16 rows (0 to 15, 16 to 31, ..., all dimensions but the last counted through in order) at most 5 rows name the same one
- gate_logits: float32 [3, 2048, 8], P(None, ('dp', 'ep')), parts along dimension 1, may hold values from -2 to 2
- w_gate_up: bfloat16 [64, 4096, 1536], P('ep'), may hold values from -0.09375 to 0.09375
- w_down: bfloat16 [64, 768, 4096], P('ep'), may hold values from -0.21875 to 0.21875
- swap_step: int32 [128], P('dp'), parts along dimension 0, may hold values from 1 to 3, as said below
Outputs:
- mixed: bfloat16 [3, 2048, 4096], P(None, ('dp', 'ep')), parts along dimension 1
- relocated_down: bfloat16 [128, 768, 4096], P(('dp', 'ep')), parts along dimension 0
There are 2 independent parts, one for each index of `dp`. A program takes and returns all parts, laid end to end along the dimension named above; an argument that names none is the same for every part. Nothing has to cross between parts.
Inputs may be any that keep to these rules, and one draw needn't show every extreme that they name: `expert_ids`: each token names 8 different experts; within one step, the 16 tokens of one device (aligned blocks) name one expert in at most 5 of their rows, and some expert in exactly 5 rows in some blocks. `swap_step`: slots 2i and 2i+1 share one value; 3 means the pair keeps its experts through the steps.
All inputs are finite; a program needn't handle non-finite values.
Results may differ from a plain program's by a relative error of at most 0.0057.
Values may be sent and summed in bfloat16 or wider, within the bound.
A program may use at most 192 MiB of HBM per device.

v0:
```python
import jax
import jax.numpy as jnp
from jax import lax
from jax.sharding import PartitionSpec as P

CAP = 5


def expert_block(rows_in, gate_up, down_proj):
    hidden_width = down_proj.shape[0]
    product = jnp.dot(rows_in, gate_up, preferred_element_type=jnp.float32)
    activated = (jax.nn.silu(product[:, :hidden_width]) * product[:, hidden_width:]).astype(
        jnp.bfloat16
    )
    return jnp.dot(activated, down_proj, preferred_element_type=jnp.float32).astype(jnp.bfloat16)


def routing(expert_ids, gate_logits, devices, slots):
    num_steps, tok_rows, _ = expert_ids.shape
    exponent = jnp.exp(gate_logits)
    weights = exponent / jnp.sum(exponent, axis=-1, keepdims=True)
    match = expert_ids[..., None] == jnp.arange(devices, dtype=jnp.int32)
    names = jnp.any(match, axis=2)
    dense_weight = jnp.sum(jnp.where(match, weights[..., None], 0.0), axis=2)
    earlier = jnp.arange(tok_rows)[:, None] > jnp.arange(tok_rows)[None, :]
    rank = jnp.sum(
        (earlier[None, :, :, None] & names[:, None, :, :]).astype(jnp.int32), axis=2
    )
    slot = rank + CAP * jnp.arange(num_steps, dtype=jnp.int32)[:, None, None]
    slot = jnp.where(names, slot, -1).reshape(num_steps * tok_rows, devices)
    onehot = slot[:, :, None] == jnp.arange(slots, dtype=jnp.int32)
    weighted = jnp.where(
        onehot, dense_weight.reshape(num_steps * tok_rows, devices)[:, :, None], 0.0
    )
    rows = num_steps * tok_rows
    return (
        onehot.astype(jnp.bfloat16).reshape(rows, devices * slots),
        weighted.reshape(rows, devices * slots),
    )


def on_device(hidden, expert_ids, gate_logits, w_gate_up, w_down, swap_step):
    devices = lax.axis_size("ep")
    my_index = lax.axis_index("ep")
    num_steps, tok_rows, model_dim = hidden.shape
    slots = 16
    pairs = [(source, source ^ 1) for source in range(devices)]
    other_down = lax.ppermute(w_down[0], "ep", pairs)
    onehot, weighted = routing(expert_ids, gate_logits, devices, slots)
    tokens = hidden.reshape(num_steps * tok_rows, model_dim)
    send = lax.dot_general(
        onehot, tokens, (((0,), (0,)), ((), ())), preferred_element_type=jnp.float32
    ).astype(jnp.bfloat16)
    received = lax.all_to_all(
        send.reshape(devices, slots, model_dim), "ep", split_axis=0, concat_axis=0, tiled=True
    )
    outputs = expert_block(
        received.reshape(devices * slots, model_dim), w_gate_up[0], w_down[0]
    )
    returned = lax.all_to_all(
        outputs.reshape(devices, slots, model_dim), "ep", split_axis=0, concat_axis=0, tiled=True
    ).reshape(devices * slots, model_dim)
    high = weighted.astype(jnp.bfloat16)
    low = (weighted - high.astype(jnp.float32)).astype(jnp.bfloat16)
    both = jnp.dot(
        jnp.concatenate([high, low], axis=0), returned, preferred_element_type=jnp.float32
    )
    rows = num_steps * tok_rows
    mixed = (both[:rows] + both[rows:]).astype(jnp.bfloat16).reshape(hidden.shape)
    relocated = jnp.where(swap_step[my_index] < num_steps, other_down, w_down[0])
    return (mixed, relocated[None])


def solution(mesh):
    in_specs = (
        P(None, ("dp", "ep"), None),
        P(None, ("dp", "ep"), None),
        P(None, ("dp", "ep"), None),
        P("ep", None, None),
        P("ep", None, None),
        P("dp"),
    )
    out_specs = (P(None, ("dp", "ep"), None), P(("dp", "ep"), None, None))
    return jax.shard_map(
        on_device, mesh=mesh, in_specs=in_specs, out_specs=out_specs, check_vma=False
    )
```

profile of v0, /device:TPU:53, one launch (start us, length us, event | category | flops | bytes accessed | tf_op | source)
XLA Modules:
  0.0 265.8 jit_solution(13446259951938177173)
XLA Ops:
  0.6 0.0 copy-start
  0.7 0.8 copy.17
  1.5 0.1 fusion.13
  1.6 0.1 add.26
  1.7 0.1 add.27
  1.8 0.2 convert_reduce_fusion
  2.0 0.1 fusion.14
  2.0 0.1 copy.18
  2.1 0.1 iota_compare_fusion
  2.2 0.0 copy-done
  2.2 2.3 convolution_convert_fusion.1
  4.5 0.0 slice-start
  4.5 106.4 %all_to_all.10 = bf16[64,16,4096]{2,1,0:T(8,128)(2,1)S(1)} all-to-all(bf16[64,16,4096]{2,1,0:T(8,128)(2,1)S(1)} %bitcast.47), channel_id=1, replica_groups=mesh['ep'=64,'dp'=2] {'ep'}, dimensions={0} | all-to-all | bytes 16777216 | tf_op jit(solution)/shard_map/all_to_all | solution.py:54
  110.9 15.8 %fusion = f32[1024,1536]{1,0:T(8,128)S(1)} fusion(bf16[1024,4096]{1,0:T(8,128)(2,1)S(1)} %bitcast.49, bf16[1,4096,1536]{2,1,0:T(8,128)(2,1)} %param.9), kind=kOutput, calls=%fused_computation | convolution fusion | flops 12884901888 | bytes 27262976 | tf_op jit(solution)/shard_map/dot_general | solution.py:11
  126.7 0.0 slice-done
  126.8 0.0 slice-done.1
  126.8 8.9 %convolution_convert_fusion = bf16[1024,4096]{1,0:T(8,128)(2,1)} fusion(f32[1024,1536]{1,0:T(8,128)S(1)} %fusion, bf16[1,768,4096]{2,1,0:T(8,128)(2,1)S(1)} %bitcast.52), kind=kOutput, calls=%fused_computation.2 | convolution fusion | flops 6451363840 | bytes 20971520 | tf_op jit(solution)/shard_map/dot_general | solution.py:15
  135.7 9.1 %all-to-all-start.1 = ((bf16[64,16,4096]{2,1,0:T(8,128)(2,1)}), bf16[64,16,4096]{2,1,0:T(8,128)(2,1)}, u32[]{:S(2)}, u32[]{:S(2)}) async-start(bf16[64,16,4096]{2,1,0:T(8,128)(2,1)} %bitcast.48), calls=%async_computation.1 | async-start | bytes 16777216 | tf_op jit(solution)/shard_map/all_to_all | solution.py:60
  144.7 0.6 collective-permute-start
  145.4 0.0 copy-done.2
  145.4 0.1 copy.19
  145.5 0.2 select_reduce_fusion
  145.7 0.1 copy.20
  145.8 0.1 eq.53
  145.8 0.2 fusion.8
  146.1 0.2 fusion.7
  146.3 0.6 dynamic_slice.3
  147.5 8.0 %collective-permute-done = bf16[768,4096]{1,0:T(8,128)(2,1)} collective-permute-done((bf16[768,4096]{1,0:T(8,128)(2,1)}, bf16[768,4096]{1,0:T(8,128)(2,1)}, u32[]{:S(2)}, u32[]{:S(2)}) %collective-permute-start) | collective-permute-done | bytes 6291488 | tf_op jit(solution)/shard_map/ppermute | solution.py:48
  155.5 6.1 %select_bitcast_fusion = bf16[1,768,4096]{2,1,0:T(8,128)(2,1)} fusion(bf16[768,4096]{1,0:T(8,128)(2,1)} %collective-permute-done, pred[]{:T(512)} %bitcast.14, bf16[1,768,4096]{2,1,0:T(8,128)(2,1)} %param.10), kind=kLoop, calls=%fused_computation.4 | loop fusion | flops 3145728 | bytes 18874368 | tf_op jit(solution)/shard_map/broadcast_in_dim | solution.py:71
  161.6 98.3 %all-to-all-done.1 = bf16[64,16,4096]{2,1,0:T(8,128)(2,1)} async-done(((bf16[64,16,4096]{2,1,0:T(8,128)(2,1)}), bf16[64,16,4096]{2,1,0:T(8,128)(2,1)}, u32[]{:S(2)}, u32[]{:S(2)}) %all-to-all-start.1) | async-done | bytes 8388640 | tf_op jit(solution)/shard_map/all_to_all | solution.py:60
  259.9 5.0 %fusion.9 = f32[96,4096]{1,0:T(8,128)S(1)} fusion(bf16[1024,4096]{1,0:T(8,128)(2,1)} %bitcast.12, bf16[48,1024]{0,1:T(8,128)(2,1)S(1)} %fusion.8, bf16[48,1024]{0,1:T(8,128)(2,1)S(1)} %fusion.7), kind=kOutput, calls=%fused_computation.17 | convolution fusion | flops 805699584 | bytes 10158080 | tf_op jit(solution)/shard_map/dot_general | solution.py:65
  264.9 0.8 fusion.5
  (12 shorter events, 0.1 us)
Async XLA Ops:
  0.6 1.6 copy-start
  4.5 122.2 %slice-start = ((s8[6291456]{0:T(1024)(128)(4,1)}), s8[4194304]{0:T(1024)(128)(4,1)S(1)}, s32[]{:S(2)}) async-start(s8[6291456]{0:T(1024)(128)(4,1)} %bitcast.51), calls=%async_computation.2 | async-start | bytes 8388608
  110.9 15.8 %slice-start.1 = ((s8[6291456]{0:T(1024)(128)(4,1)}), s8[2097152]{0:T(1024)(128)(4,1)S(1)}, s32[]{:S(2)}) async-start(s8[6291456]{0:T(1024)(128)(4,1)} %bitcast.51), calls=%async_computation.3 | async-start | bytes 4194304
  135.7 9.7 %copy-start.2 = (f32[3,16,8]{1,2,0:T(8,128)S(1)}, f32[3,16,8]{1,2,0:T(8,128)}, u32[]{:S(2)}) copy-start(f32[3,16,8]{1,2,0:T(8,128)} %param.8) | copy-start | bytes 4612
  135.7 10.6 %copy-start.3 = (s32[64]{0:T(128)S(1)}, s32[64]{0:T(128)}, u32[]{:S(2)}) copy-start(s32[64]{0:T(128)} %param.11) | copy-start | bytes 772
  135.7 124.2 %all-to-all-start.1 = ((bf16[64,16,4096]{2,1,0:T(8,128)(2,1)}), bf16[64,16,4096]{2,1,0:T(8,128)(2,1)}, u32[]{:S(2)}, u32[]{:S(2)}) async-start(bf16[64,16,4096]{2,1,0:T(8,128)(2,1)} %bitcast.48), calls=%async_computation.1 | async-start | bytes 16777216 | tf_op jit(solution)/shard_map/all_to_all | solution.py:60
  144.7 10.8 %collective-permute-start = (bf16[768,4096]{1,0:T(8,128)(2,1)}, bf16[768,4096]{1,0:T(8,128)(2,1)}, u32[]{:S(2)}, u32[]{:S(2)}) collective-permute-start(bf16[768,4096]{1,0:T(8,128)(2,1)} %bitcast.50), channel_id=1, source_target_pairs={{0,2},{2,0},{4,6},{6,4},{8,10},{10,8},{12,14},{14,12},{16,18},{18,... | collective-permute-start | bytes 18874376 | tf_op jit(solution)/shard_map/ppermute | solution.py:48
  259.9 5.8 %copy-start.1 = (bf16[3,16,4096]{2,1,0:T(8,128)(2,1)S(1)}, bf16[3,16,4096]{2,1,0:T(8,128)(2,1)}, u32[]{:S(2)}) copy-start(bf16[3,16,4096]{2,1,0:T(8,128)(2,1)} %param.6) | copy-start | bytes 1179652
where the time goes:
time: 266 us
  blocking collectives  106 us (40%)
  waiting for transfers between devices  106 us (40%)
  matrix products  32 us (12%)
  starting transfers between devices  9.7 us (4%)
  other arithmetic  8.06 us (3%)
    all_to_all x1, blocking collectives, on_device(): lax.all_to_all(send.reshape(devices, slots, model_dim), 'ep', split_axis=...  106 us
    all_to_all x1, waiting for transfers between devices, on_device(): lax.all_to_all(outputs.reshape(devices, slots, model_dim), 'ep', split_ax...  98.3 us
    dot_general x1, matrix products, expert_block(): product = jnp.dot(rows_in, gate_up, preferred_element_type=jnp.float32)  15.8 us
    all_to_all x1, starting transfers between devices, on_device(): lax.all_to_all(outputs.reshape(devices, slots, model_dim), 'ep', split_ax...  9.08 us
    dot_general x1, matrix products, expert_block(): jnp.dot(activated, down_proj, preferred_element_type=jnp.float32)  8.88 us
    ppermute x1, waiting for transfers between devices, on_device(): other_down = lax.ppermute(w_down[0], 'ep', pairs)  7.99 us
    broadcast_in_dim x1, other arithmetic, on_device(): return (mixed, relocated[None])  6.14 us
  transfers between devices with their start and end apart: 2, of which 2 were waited for; matrix products, arithmetic and copies ran while one was open for 3% of the time, Pallas kernels for 0%

commit v1 on v0

v1 whole, which is shorter than its diff:
```python
import functools

import jax
import jax.numpy as jnp
from jax import lax
from jax.experimental import pallas as pl
from jax.experimental.pallas import tpu as pltpu
from jax.sharding import PartitionSpec as P

CAP = 5
STEPS = 3
TOK = 16
RING = 4
BLOCKS = 32
GROUP = 16
META = 128
OWN, OTHER = 0, 1
UP, DOWN = 0, 1
OFFSETS = (0, 3, 1, 2)
BF16 = jnp.bfloat16
F32 = jnp.float32


def moe_kernel(
    expert_ref, tok_a, tok_b, wgu_hbm, wd_hbm, out_ref,
    gath_a, gath_b, rbuf_a, rbuf_b, wgu, wd, picked, pick_send, out_own, out_send, out_recv,
    act, weight_hi, weight_lo,
    ag_send, ag_recv, rs_send, rs_recv, pair_send, pair_recv, load_sem,
):
    half = tok_b.shape[1]
    hidden_width = wd.shape[0]
    gath = (gath_a, gath_b)
    rbuf = (rbuf_a, rbuf_b)
    tok = (tok_a, tok_b)
    me = lax.axis_index("ep")
    my_dp = lax.axis_index("dp")
    core = me % 2
    xh = (me // 2) % 2
    y = (me // 4) % RING
    z = me // 16

    def device(zz, yy, xx, dp):
        return {"ep": ((zz * RING + yy) * 2 + xx) * 2 + core, "dp": dp}

    x_partner = device(z, y, 1 - xh, 1 - my_dp)
    core_partner = {"ep": me + 1 - 2 * core, "dp": my_dp}
    first = (z, y)
    second = (y, z)

    def place(h, f, g):
        return (f, g) if h == 0 else (g, f)

    def block(h, f, g, kind):
        zz, yy = place(h, f, g)
        xx = xh if kind == OWN else 1 - xh
        start = ((zz * RING + yy) * 2 + xx) * TOK
        return pl.ds(pl.multiple_of(start, TOK), TOK)

    def shifted(value, amount):
        return (value + amount) % RING

    def first_to(h, way):
        f = shifted(first[h], 1 if way == UP else 3)
        zz, yy = place(h, f, second[h])
        return device(zz, yy, xh, my_dp)

    def second_to(h, way):
        g = shifted(second[h], 1 if way == UP else 3)
        zz, yy = place(h, first[h], g)
        return device(zz, yy, xh, my_dp)

    def remote(src, dst, send, recv, to):
        return pltpu.make_async_remote_copy(
            src_ref=src, dst_ref=dst, send_sem=send, recv_sem=recv,
            device_id=to, device_id_type=pl.DeviceIdType.MESH,
        )

    loads = (
        pltpu.make_async_copy(wgu_hbm, wgu, load_sem.at[0]),
        pltpu.make_async_copy(wd_hbm, wd, load_sem.at[1]),
    )

    barrier = pltpu.get_barrier_semaphore()
    friends = [x_partner, core_partner] + [
        to(0, way) for to in (first_to, second_to) for way in (UP, DOWN)
    ]
    for friend in friends:
        pl.semaphore_signal(
            barrier, inc=1, device_id=friend, device_id_type=pl.DeviceIdType.MESH
        )
    pl.semaphore_wait(barrier, len(friends))

    ag_started = {}

    def ag_copy(h, s, idx, rows, to, from_input=False):
        source = (
            tok[h].at[pl.ds(s * TOK, TOK), :] if from_input else gath[h].at[s, rows, :]
        )
        return remote(
            source, gath[h].at[s, rows, :], ag_send.at[h, s, idx], ag_recv.at[h, s, idx], to
        )

    def ag_start(h, s, idx, rows, to, from_input=False):
        copy = ag_copy(h, s, idx, rows, to, from_input)
        copy.start()
        ag_started.setdefault(s, []).append(copy)

    def ag_wait(h, s, idx, rows):
        ag_copy(h, s, idx, rows, x_partner).wait_recv()

    def ag_actions(h, s):
        f, g = first[h], second[h]
        f_of = [shifted(f, off) for off in OFFSETS]

        def spread(j, kind, from_input=False):
            for way in (UP, DOWN):
                ag_start(
                    h, s, 7 + way * 8 + j * 2 + kind, block(h, f_of[j], g, kind),
                    second_to(h, way), from_input,
                )

        def init():
            mine = block(h, f, g, OWN)
            ag_start(h, s, 0, mine, x_partner, True)
            for way in (UP, DOWN):
                ag_start(h, s, 1 + way * 2 + OWN, mine, first_to(h, way), True)
            gath[h][s, mine, :] = tok[h][pl.ds(s * TOK, TOK), :]

        def init2():
            spread(0, OWN, True)

        def a1():
            theirs = block(h, f, g, OTHER)
            ag_wait(h, s, 0, theirs)
            for way in (UP, DOWN):
                ag_start(h, s, 1 + way * 2 + OTHER, theirs, first_to(h, way))
            spread(0, OTHER)

        def near(way, kind):
            j = 1 if way == UP else 2
            rows = block(h, f_of[j], g, kind)
            ag_wait(h, s, 1 + way * 2 + kind, rows)
            if (way, kind) == (UP, OWN) or (way, kind) == (DOWN, OTHER):
                ag_start(h, s, 5 + way, rows, first_to(h, way))
            spread(j, kind)

        def far(way):
            kind = OWN if way == UP else OTHER
            ag_wait(h, s, 5 + way, block(h, f_of[3], g, kind))
            spread(3, kind)

        def forward(j, kind):
            way = UP if kind == OWN else DOWN
            rows = block(h, f_of[j], shifted(g, 3 if way == UP else 1), kind)
            ag_wait(h, s, 7 + way * 8 + j * 2 + kind, rows)
            ag_start(h, s, 23 + way * 4 + j, rows, second_to(h, way))

        def last(j):
            ag_wait(h, s, 7 + DOWN * 8 + j * 2 + OWN, block(h, f_of[j], shifted(g, 1), OWN))
            ag_wait(h, s, 7 + UP * 8 + j * 2 + OTHER, block(h, f_of[j], shifted(g, 3), OTHER))
            ag_wait(h, s, 23 + UP * 4 + j, block(h, f_of[j], shifted(g, 2), OWN))
            ag_wait(h, s, 23 + DOWN * 4 + j, block(h, f_of[j], shifted(g, 2), OTHER))

        part = functools.partial
        head = [init, init2]
        body = [
            a1, part(near, UP, OWN), part(near, DOWN, OWN), part(forward, 0, OWN),
            part(near, UP, OTHER), part(near, DOWN, OTHER), part(forward, 0, OTHER),
            part(far, UP), part(far, DOWN),
            part(forward, 1, OWN), part(forward, 2, OWN),
            part(forward, 1, OTHER), part(forward, 2, OTHER),
            part(forward, 3, OWN), part(forward, 3, OTHER),
        ]
        tail = [part(last, j) for j in (0, 1, 2, 3)]
        return head, body, tail

    def both(make, s):
        a, b = make(0, s), make(1, s)
        return [
            [act_ for pair in zip(pa, pb) for act_ in pair] for pa, pb in zip(a, b)
        ]

    chunk = min(512, half)
    act_chunk = min(256, hidden_width)

    def routing(s, grp):
        meta = gath_a[s, pl.ds(grp * 256, 256), pl.ds(half, META)].astype(F32)
        lane = lax.broadcasted_iota(jnp.int32, (256, META), 1)
        row = lax.broadcasted_iota(jnp.int32, (256, 256), 0)
        col = lax.broadcasted_iota(jnp.int32, (256, 256), 1)
        lower = jnp.where(
            (row > col) & (row // TOK == col // TOK), 1.0, 0.0
        ).astype(BF16)
        base = ((row // TOK) * CAP).astype(F32)
        colf = col.astype(F32)
        slot = jnp.zeros((256, 256), F32)
        hi = jnp.zeros((256, 256), F32)
        lo = jnp.zeros((256, 256), F32)
        shifted_hi = pltpu.roll(meta, META - 8, axis=1)
        shifted_lo = pltpu.roll(meta, META - 16, axis=1)
        for kind in (0, 1):
            expert = expert_ref[kind]
            match = (meta == expert) & (lane < 8)
            names = jnp.sum(jnp.where(match, 1.0, 0.0), axis=1, keepdims=True)
            w_hi = jnp.sum(jnp.where(match, shifted_hi, 0.0), axis=1, keepdims=True)
            w_lo = jnp.sum(jnp.where(match, shifted_lo, 0.0), axis=1, keepdims=True)
            rank = jnp.dot(
                lower, jnp.broadcast_to(names, (256, 256)).astype(BF16),
                preferred_element_type=F32,
            )
            target = base + rank + float(kind * GROUP * CAP)
            here = jnp.where((colf == target) & (names > 0.5), 1.0, 0.0)
            slot += here
            hi += here * w_hi
            lo += here * w_lo
        weight_hi[grp] = hi.astype(BF16)
        weight_lo[grp] = lo.astype(BF16)
        return slot.T.astype(BF16)[: 2 * GROUP * CAP, :]

    group_rows = GROUP * CAP
    own_rows = 2 * group_rows

    def select(s, grp):
        onehot = routing(s, grp)
        for h in (0, 1):
            for c in range(half // chunk):
                got = jnp.dot(
                    onehot,
                    gath[h][s, pl.ds(grp * 256, 256), pl.ds(c * chunk, chunk)],
                    preferred_element_type=F32,
                ).astype(BF16)
                at = pl.ds(h * half + c * chunk, chunk)
                picked[s, pl.ds(grp * group_rows, group_rows), at] = got[:group_rows]
                pick_send[s % 2, pl.ds(grp * group_rows, group_rows), at] = got[group_rows:]

    def pick_copy(s):
        return remote(
            pick_send.at[s % 2], picked.at[s, pl.ds(own_rows, own_rows), :],
            pair_send.at[0, s], pair_recv.at[0, s], core_partner,
        )

    def back_copy(s):
        return remote(
            out_send.at[s % 2], out_recv.at[s], pair_send.at[1, s], pair_recv.at[1, s],
            core_partner,
        )

    def ffn_up(s, c):
        rows = picked[s]
        gate = jnp.dot(rows, wgu[:, pl.ds(c * act_chunk, act_chunk)], preferred_element_type=F32)
        up = jnp.dot(
            rows, wgu[:, pl.ds(hidden_width + c * act_chunk, act_chunk)],
            preferred_element_type=F32,
        )
        act[:, pl.ds(c * act_chunk, act_chunk)] = (
            gate / (1.0 + jnp.exp(-gate)) * up
        ).astype(BF16)

    def ffn_down(s, c):
        at = pl.ds(c * chunk, chunk)
        got = jnp.dot(act[...], wd[:, at], preferred_element_type=F32).astype(BF16)
        out_own[:, at] = got[:own_rows]
        out_send[s % 2, :, at] = got[own_rows:]

    def partial_sums(s, grp, c):
        rows = pl.ds(grp * group_rows, group_rows)
        h, offset = divmod(c * chunk, half)
        at = pl.ds(c * chunk, chunk)
        outs = jnp.concatenate([out_own[rows, at], out_recv[s, rows, at]], axis=0)
        total = jnp.dot(
            weight_hi[grp, :, : 2 * group_rows], outs, preferred_element_type=F32
        ) + jnp.dot(weight_lo[grp, :, : 2 * group_rows], outs, preferred_element_type=F32)
        gath[h][s, pl.ds(grp * 256, 256), pl.ds(offset, chunk)] = total.astype(BF16)

    def expert_actions(s):
        part = functools.partial
        actions = []
        if s == 0:
            actions.append(lambda: [load.wait() for load in loads])
        actions += [part(select, s, 0), part(select, s, 1)]
        actions.append(lambda: pick_copy(s).start())
        actions.append(lambda: [copy.wait_send() for copy in ag_started[s]])
        actions.append(lambda: pick_copy(s).wait())
        actions += [part(ffn_up, s, c) for c in range(hidden_width // act_chunk)]
        actions += [part(ffn_down, s, c) for c in range(2 * half // chunk)]
        actions.append(lambda: back_copy(s).start())
        actions.append(lambda: back_copy(s).wait())
        actions += [
            part(partial_sums, s, grp, c) for grp in (0, 1) for c in range(2 * half // chunk)
        ]
        return actions

    rs_started = []

    def slot_ref(h, s, idx):
        return rbuf[h].at[s, pl.ds(idx * TOK, TOK), :]

    def rs_copy(h, s, idx, rows, to):
        return remote(
            gath[h].at[s, rows, pl.ds(0, half)], slot_ref(h, s, idx),
            rs_send.at[h, s, idx], rs_recv.at[h, s, idx], to,
        )

    def rs_actions(h, s):
        f, g = first[h], second[h]
        f_of = [shifted(f, off) for off in OFFSETS]

        def start(idx, rows, to):
            copy = rs_copy(h, s, idx, rows, to)
            copy.start()
            rs_started.append(copy)

        def wait(idx):
            rs_copy(h, s, idx, block(h, f, g, OWN), x_partner).wait_recv()

        def value(rows, slots):
            total = gath[h][s, rows, pl.ds(0, half)].astype(F32)
            for idx in slots:
                total += rbuf[h][s, pl.ds(idx * TOK, TOK), :].astype(F32)
            return total.astype(BF16)

        def store(rows, slots):
            gath[h][s, rows, pl.ds(0, half)] = value(rows, slots)

        def init_far(j):
            start(UP * 4 + j, block(h, f_of[j], shifted(g, 2), OWN), second_to(h, UP))
            start(DOWN * 4 + j, block(h, f_of[j], shifted(g, 2), OTHER), second_to(h, DOWN))

        def init_near(j):
            start(
                8 + UP * 8 + j * 2 + OTHER, block(h, f_of[j], shifted(g, 1), OTHER),
                second_to(h, UP),
            )
            start(
                8 + DOWN * 8 + j * 2 + OWN, block(h, f_of[j], shifted(g, 3), OWN),
                second_to(h, DOWN),
            )

        def add(j):
            up_rows = block(h, f_of[j], shifted(g, 1), OWN)
            down_rows = block(h, f_of[j], shifted(g, 3), OTHER)
            wait(UP * 4 + j)
            store(up_rows, [UP * 4 + j])
            wait(DOWN * 4 + j)
            store(down_rows, [DOWN * 4 + j])
            start(8 + UP * 8 + j * 2 + OWN, up_rows, second_to(h, UP))
            start(8 + DOWN * 8 + j * 2 + OTHER, down_rows, second_to(h, DOWN))

        def arrived(j, kind):
            slots = [8 + way * 8 + j * 2 + kind for way in (UP, DOWN)]
            for idx in slots:
                wait(idx)
            return slots

        def reduced(j, kind, extra, idx, way):
            slots = arrived(j, kind)
            for more in extra:
                wait(more)
            rows = block(h, f_of[j], g, kind)
            store(rows, slots + extra)
            start(idx, rows, first_to(h, way))

        def to_x():
            slots = arrived(0, OTHER) + [26 + UP * 2 + OTHER, 26 + DOWN * 2 + OTHER]
            for idx in slots[2:]:
                wait(idx)
            rows = block(h, f, g, OTHER)
            store(rows, slots)
            start(30, rows, x_partner)

        def finish():
            slots = arrived(0, OWN) + [26 + UP * 2 + OWN, 26 + DOWN * 2 + OWN, 30]
            for idx in slots[2:]:
                wait(idx)
            out_ref[pl.ds(s * TOK, TOK), pl.ds(h * half, half)] = value(
                block(h, f, g, OWN), slots
            )

        part = functools.partial
        order = (3, 2, 1, 0)
        head = [part(init_far, j) for j in order] + [part(init_near, j) for j in order]
        body = [part(add, j) for j in order]
        body += [
            part(reduced, 3, OWN, [], 24 + UP, UP),
            part(reduced, 3, OTHER, [], 24 + DOWN, DOWN),
            part(reduced, 2, OTHER, [], 26 + UP * 2 + OTHER, UP),
            part(reduced, 1, OWN, [], 26 + DOWN * 2 + OWN, DOWN),
            part(reduced, 2, OWN, [24 + UP], 26 + UP * 2 + OWN, UP),
            part(reduced, 1, OTHER, [24 + DOWN], 26 + DOWN * 2 + OTHER, DOWN),
            to_x,
        ]
        tail = [finish]
        return head, body, tail

    def run(actions):
        for action in actions:
            action()

    def blend(*lists):
        total = max(len(one) for one in lists)
        merged = []
        for index, one in enumerate(lists):
            for at, action in enumerate(one):
                merged.append(((at + 0.5) / len(one), index, at, action))
        merged.sort(key=lambda item: item[:3])
        return [item[3] for item in merged]

    ag = [both(ag_actions, s) for s in range(STEPS)]
    rs = [both(rs_actions, s) for s in range(STEPS)]
    ex = [expert_actions(s) for s in range(STEPS)]

    run(ag[0][0])
    for load in loads:
        load.start()
    run(ag[0][1])
    run(ag[1][0])
    run(ag[0][2])
    run(blend(ag[1][1], ex[0]))
    run(ag[2][0])
    run(rs[0][0])
    run(ag[1][2])
    run(blend(ag[2][1], ex[1], rs[0][1]))
    run(rs[1][0])
    run(ag[2][2])
    run(rs[0][2])
    run(blend(ex[2], rs[1][1]))
    run(rs[2][0])
    run(rs[1][2])
    run(rs[2][1])
    run(rs[2][2])
    for copy in rs_started:
        copy.wait_send()


def moe(experts, tok_a, tok_b, wgu, wd):
    rows, half = tok_b.shape
    depth, wide = wgu.shape
    hidden_width = wd.shape[0]
    vmem = pltpu.VMEM
    group_rows = GROUP * CAP
    own_rows = 2 * group_rows
    dma = pltpu.SemaphoreType.DMA
    return pl.pallas_call(
        moe_kernel,
        out_shape=jax.ShapeDtypeStruct((rows, 2 * half), BF16),
        in_specs=[
            pl.BlockSpec(memory_space=pltpu.SMEM),
            pl.BlockSpec(memory_space=vmem),
            pl.BlockSpec(memory_space=vmem),
            pl.BlockSpec(memory_space=pl.ANY),
            pl.BlockSpec(memory_space=pl.ANY),
        ],
        out_specs=pl.BlockSpec(memory_space=vmem),
        scratch_shapes=[
            vmem((STEPS, BLOCKS * TOK, half + META), BF16),
            vmem((STEPS, BLOCKS * TOK, half), BF16),
            vmem((STEPS, 31 * TOK, half), BF16),
            vmem((STEPS, 31 * TOK, half), BF16),
            vmem((depth, wide), BF16),
            vmem((hidden_width, depth), BF16),
            vmem((STEPS, 2 * own_rows, depth), BF16),
            vmem((2, own_rows, depth), BF16),
            vmem((own_rows, depth), BF16),
            vmem((2, own_rows, depth), BF16),
            vmem((STEPS, own_rows, depth), BF16),
            vmem((2 * own_rows, hidden_width), BF16),
            vmem((2, 256, 256), BF16),
            vmem((2, 256, 256), BF16),
            dma((2, STEPS, 31)),
            dma((2, STEPS, 31)),
            dma((2, STEPS, 31)),
            dma((2, STEPS, 31)),
            dma((2, STEPS)),
            dma((2, STEPS)),
            dma((2,)),
        ],
        compiler_params=pltpu.CompilerParams(
            collective_id=0, has_side_effects=True, vmem_limit_bytes=67043328
        ),
    )(experts, tok_a, tok_b, wgu, wd)


def on_device(hidden, expert_ids, gate_logits, w_gate_up, w_down, swap_step):
    devices = lax.axis_size("ep")
    my_index = lax.axis_index("ep")
    num_steps, tok_rows, model_dim = hidden.shape
    rows = num_steps * tok_rows
    pairs = [(source, source ^ 1) for source in range(devices)]
    other_down = lax.ppermute(w_down[0], "ep", pairs)

    exponent = jnp.exp(gate_logits)
    weights = exponent / jnp.sum(exponent, axis=-1, keepdims=True)
    high = lax.reduce_precision(weights, 8, 7)
    low = weights - high
    meta = jnp.concatenate([expert_ids.astype(F32), high, low], axis=-1).reshape(rows, -1)
    meta = jnp.pad(meta, ((0, 0), (0, META - meta.shape[1]))).astype(BF16)
    tokens = hidden.reshape(rows, model_dim)
    half = model_dim // 2
    experts = jnp.stack([my_index, my_index ^ 1]).astype(F32)
    mixed = moe(
        experts,
        jnp.concatenate([tokens[:, :half], meta], axis=1),
        tokens[:, half:],
        w_gate_up[0],
        w_down[0],
    )
    relocated = jnp.where(swap_step[my_index] < num_steps, other_down, w_down[0])
    return (mixed.reshape(hidden.shape), relocated[None])


def solution(mesh):
    in_specs = (
        P(None, ("dp", "ep"), None),
        P(None, ("dp", "ep"), None),
        P(None, ("dp", "ep"), None),
        P("ep", None, None),
        P("ep", None, None),
        P("dp"),
    )
    out_specs = (P(None, ("dp", "ep"), None), P(("dp", "ep"), None, None))
    return jax.shard_map(
        on_device, mesh=mesh, in_specs=in_specs, out_specs=out_specs, check_vma=False
    )
```

time: 266 us -> 182 us (0.68)
  the two profiles are of different devices: /device:TPU:53 before, /device:TPU:0 now
where the time goes in v1:
time: 182 us
  Pallas kernels  166 us (91%)
  other arithmetic  10.8 us (6%)
  local copies, waits for them, and re-layouts  3.8 us (2%)
    pallas_call x1, Pallas kernels, moe(): pl.pallas_call(moe_kernel, out_shape=jax.ShapeDtypeStruct((rows, 2 * half...  166 us
    broadcast_in_dim x1, other arithmetic, on_device(): return (mixed.reshape(hidden.shape), relocated[None])  8.01 us
  transfers between devices with their start and end apart: 1, of which 0 were waited for; matrix products, arithmetic and copies ran while one was open for 3% of the time, Pallas kernels for 91%

profile of v1, /device:TPU:0, one launch (start us, length us, event | category | flops | bytes accessed | tf_op | source)
XLA Modules:
  0.0 182.0 jit_solution(5923250619571646504)
XLA Ops:
  0.6 0.1 collective-permute-start
  0.7 0.7 convert_convert_fusion
  1.4 0.7 reduce-precision_convert_fusion
  2.2 0.1 copy.8
  2.3 0.7 add_convert_fusion.expert_ref
  2.9 1.7 fusion.6
  4.7 0.7 fusion.3.tok_a
  5.4 165.9 %shard_map.77 = bf16[48,4096]{1,0:T(8,128)(2,1)} custom-call(f32[2]{0:T(128)} %add_convert_fusion.expert_ref, bf16[48,2176]{1,0:T(8,128)(2,1)} %fusion.3.tok_a, bf16[48,2048]{1,0:T(8,128)(2,1)} %get-tuple-element.2.tok_b, bf16[4096,1536]{1,0:T(8,128)(2,1)} %bitcast.13, bf16[768,4096]{1,0:T(8,128)(2,1)} %bitcast.12), custom_call_target="tpu_custom_call" | custom-call | tf_op jit(solution)/shard_map/pallas_call | solution.py:443
  171.3 1.2 dynamic_slice.3
  173.2 0.0 collective-permute-done
  173.2 0.0 copy-start
  173.2 8.0 %select_bitcast_fusion = bf16[1,768,4096]{2,1,0:T(8,128)(2,1)} fusion(bf16[768,4096]{1,0:T(8,128)(2,1)} %collective-permute-done, pred[]{:T(512)} %bitcast.7, bf16[1,768,4096]{2,1,0:T(8,128)(2,1)} %param.10), kind=kLoop, calls=%fused_computation.1 | loop fusion | flops 3145728 | bytes 18874368 | tf_op jit(solution)/shard_map/broadcast_in_dim | solution.py:508
  181.2 0.0 copy-done
  181.2 0.7 copy.10
  (1 shorter events, 0.0 us)
Async XLA Ops:
  0.6 172.6 %collective-permute-start = (bf16[768,4096]{1,0:T(8,128)(2,1)}, bf16[768,4096]{1,0:T(8,128)(2,1)}, u32[]{:S(2)}, u32[]{:S(2)}) collective-permute-start(bf16[768,4096]{1,0:T(8,128)(2,1)} %bitcast.11), channel_id=1, source_target_pairs={{0,2},{2,0},{4,6},{6,4},{8,10},{10,8},{12,14},{14,12},{16,18},{18,... | collective-permute-start | bytes 18874376 | tf_op jit(solution)/shard_map/ppermute | solution.py:489
  173.2 8.0 %copy-start = (bf16[48,4096]{1,0:T(8,128)(2,1)S(1)}, bf16[48,4096]{1,0:T(8,128)(2,1)}, u32[]{:S(2)}) copy-start(bf16[48,4096]{1,0:T(8,128)(2,1)} %shard_map.77) | copy-start | bytes 1179652

commit v2 on v1

--- a/solution.py
+++ b/solution.py
@@ -16,22 +16,23 @@
 META = 128
 OWN, OTHER = 0, 1
 UP, DOWN = 0, 1
+LAG = 2
 OFFSETS = (0, 3, 1, 2)
 BF16 = jnp.bfloat16
 F32 = jnp.float32
 
 
 def moe_kernel(
-    expert_ref, tok_a, tok_b, wgu_hbm, wd_hbm, out_ref,
+    expert_ref, tok_a, tokens_ref, wgu_hbm, wd_hbm, out_ref,
     gath_a, gath_b, rbuf_a, rbuf_b, wgu, wd, picked, pick_send, out_own, out_send, out_recv,
     act, weight_hi, weight_lo,
     ag_send, ag_recv, rs_send, rs_recv, pair_send, pair_recv, load_sem,
 ):
-    half = tok_b.shape[1]
+    half = tokens_ref.shape[1] // 2
     hidden_width = wd.shape[0]
     gath = (gath_a, gath_b)
     rbuf = (rbuf_a, rbuf_b)
-    tok = (tok_a, tok_b)
+    tok = (tok_a, tokens_ref.at[:, pl.ds(half, half)])
     me = lax.axis_index("ep")
     my_dp = lax.axis_index("dp")
     core = me % 2
@@ -232,17 +233,21 @@
                 at = pl.ds(h * half + c * chunk, chunk)
                 picked[s, pl.ds(grp * group_rows, group_rows), at] = got[:group_rows]
                 pick_send[s % 2, pl.ds(grp * group_rows, group_rows), at] = got[group_rows:]
-
-    def pick_copy(s):
+            pick_copy(s, grp, h).start()
+
+    def pick_copy(s, grp, h):
+        at = pl.ds(h * half, half)
         return remote(
-            pick_send.at[s % 2], picked.at[s, pl.ds(own_rows, own_rows), :],
-            pair_send.at[0, s], pair_recv.at[0, s], core_partner,
-        )
-
-    def back_copy(s):
+            pick_send.at[s % 2, pl.ds(grp * group_rows, group_rows), at],
+            picked.at[s, pl.ds(own_rows + grp * group_rows, group_rows), at],
+            pair_send.at[0, s, grp * 2 + h], pair_recv.at[0, s, grp * 2 + h], core_partner,
+        )
+
+    def back_copy(s, c):
+        at = pl.ds(c * chunk, chunk)
         return remote(
-            out_send.at[s % 2], out_recv.at[s], pair_send.at[1, s], pair_recv.at[1, s],
-            core_partner,
+            out_send.at[s % 2, :, at], out_recv.at[s, :, at],
+            pair_send.at[1, s, c], pair_recv.at[1, s, c], core_partner,
         )
 
     def ffn_up(s, c):
@@ -261,6 +266,7 @@
         got = jnp.dot(act[...], wd[:, at], preferred_element_type=F32).astype(BF16)
         out_own[:, at] = got[:own_rows]
         out_send[s % 2, :, at] = got[own_rows:]
+        back_copy(s, c).start()
 
     def partial_sums(s, grp, c):
         rows = pl.ds(grp * group_rows, group_rows)
@@ -274,20 +280,25 @@
 
     def expert_actions(s):
         part = functools.partial
-        actions = []
+        chunks = 2 * half // chunk
+        lag = min(LAG, chunks)
+        actions = [part(select, s, 0), part(select, s, 1)]
         if s == 0:
             actions.append(lambda: [load.wait() for load in loads])
-        actions += [part(select, s, 0), part(select, s, 1)]
-        actions.append(lambda: pick_copy(s).start())
         actions.append(lambda: [copy.wait_send() for copy in ag_started[s]])
-        actions.append(lambda: pick_copy(s).wait())
+        actions.append(
+            lambda: [pick_copy(s, grp, h).wait() for grp in (0, 1) for h in (0, 1)]
+        )
         actions += [part(ffn_up, s, c) for c in range(hidden_width // act_chunk)]
-        actions += [part(ffn_down, s, c) for c in range(2 * half // chunk)]
-        actions.append(lambda: back_copy(s).start())
-        actions.append(lambda: back_copy(s).wait())
-        actions += [
-            part(partial_sums, s, grp, c) for grp in (0, 1) for c in range(2 * half // chunk)
-        ]
+        for c in range(chunks + lag):
+            if c < chunks:
+                actions.append(part(ffn_down, s, c))
+            if c >= lag:
+                actions.append(lambda c=c: back_copy(s, c - lag).wait())
+                actions += [part(partial_sums, s, grp, c - lag) for grp in (0, 1)]
+                for h in (0, 1):
+                    if (c - lag + 1) * chunk == (h + 1) * half:
+                        actions.append(part(run, rs_parts[s][h][0]))
         return actions
 
     rs_started = []
@@ -406,7 +417,11 @@
         return [item[3] for item in merged]
 
     ag = [both(ag_actions, s) for s in range(STEPS)]
-    rs = [both(rs_actions, s) for s in range(STEPS)]
+    rs_parts = [[rs_actions(h, s) for h in (0, 1)] for s in range(STEPS)]
+    rs = [
+        [[act_ for pair in zip(pa, pb) for act_ in pair] for pa, pb in zip(*parts)]
+        for parts in rs_parts
+    ]
     ex = [expert_actions(s) for s in range(STEPS)]
 
     run(ag[0][0])
@@ -415,16 +430,12 @@
     run(ag[0][1])
     run(ag[1][0])
     run(ag[0][2])
-    run(blend(ag[1][1], ex[0]))
-    run(ag[2][0])
-    run(rs[0][0])
+    run(blend(ag[1][1] + ag[2][0], ex[0]))
     run(ag[1][2])
     run(blend(ag[2][1], ex[1], rs[0][1]))
-    run(rs[1][0])
     run(ag[2][2])
     run(rs[0][2])
     run(blend(ex[2], rs[1][1]))
-    run(rs[2][0])
     run(rs[1][2])
     run(rs[2][1])
     run(rs[2][2])
@@ -432,8 +443,8 @@
         copy.wait_send()
 
 
-def moe(experts, tok_a, tok_b, wgu, wd):
-    rows, half = tok_b.shape
+def moe(experts, tok_a, tokens, wgu, wd):
+    rows, half = tokens.shape[0], tokens.shape[1] // 2
     depth, wide = wgu.shape
     hidden_width = wd.shape[0]
     vmem = pltpu.VMEM
@@ -470,14 +481,14 @@
             dma((2, STEPS, 31)),
             dma((2, STEPS, 31)),
             dma((2, STEPS, 31)),
-            dma((2, STEPS)),
-            dma((2, STEPS)),
+            dma((2, STEPS, 8)),
+            dma((2, STEPS, 8)),
             dma((2,)),
         ],
         compiler_params=pltpu.CompilerParams(
             collective_id=0, has_side_effects=True, vmem_limit_bytes=67043328
         ),
-    )(experts, tok_a, tok_b, wgu, wd)
+    )(experts, tok_a, tokens, wgu, wd)
 
 
 def on_device(hidden, expert_ids, gate_logits, w_gate_up, w_down, swap_step):
@@ -500,7 +511,7 @@
     mixed = moe(
         experts,
         jnp.concatenate([tokens[:, :half], meta], axis=1),
-        tokens[:, half:],
+        tokens,
         w_gate_up[0],
         w_down[0],
     )

time: 182 us -> 199 us (1.093)
  Pallas kernels: 166 us -> 184 us
    pallas_call x1, Pallas kernels: 166 us -> 184 us  [moe(): pl.pallas_call(moe_kernel, out_shape=jax.ShapeDtypeStruct((rows, 2 * half...]
  transfers between devices with their start and end apart: 1 -> 1, of which waited for: 0 -> 0; matrix products, arithmetic and copies ran while one was open for 3% -> 3% of each run, Pallas kernels for 91% -> 92%
where the time goes in v2:
time: 199 us
  Pallas kernels  184 us (92%)
  other arithmetic  10.8 us (5%)
  local copies, waits for them, and re-layouts  3.02 us (2%)
    pallas_call x1, Pallas kernels, moe(): pl.pallas_call(moe_kernel, out_shape=jax.ShapeDtypeStruct((rows, 2 * half...  184 us
    broadcast_in_dim x1, other arithmetic, on_device(): return (mixed.reshape(hidden.shape), relocated[None])  8.01 us
  transfers between devices with their start and end apart: 1, of which 0 were waited for; matrix products, arithmetic and copies ran while one was open for 3% of the time, Pallas kernels for 92%

profile of v2, /device:TPU:0, one launch (start us, length us, event | category | flops | bytes accessed | tf_op | source)
XLA Modules:
  0.0 199.0 jit_solution(9763015815663485954)
XLA Ops:
  0.6 0.1 collective-permute-start
  0.7 0.7 convert_convert_fusion
  1.4 0.7 reduce-precision_convert_fusion
  2.2 0.1 copy.8
  2.3 0.9 slice.4
  3.2 0.6 add_convert_fusion.expert_ref
  3.8 0.7 fusion.3.tok_a
  4.5 183.7 %shard_map.77 = bf16[48,4096]{1,0:T(8,128)(2,1)} custom-call(f32[2]{0:T(128)} %add_convert_fusion.expert_ref, bf16[48,2176]{1,0:T(8,128)(2,1)} %fusion.3.tok_a, bf16[48,4096]{1,0:T(8,128)(2,1)} %bitcast.16, bf16[4096,1536]{1,0:T(8,128)(2,1)} %bitcast.13, bf16[768,4096]{1,0:T(8,128)(2,1)} %bitcast.12), custom_call_target="tpu_custom_call" | custom-call | tf_op jit(solution)/shard_map/pallas_call | solution.py:454
  188.3 1.2 dynamic_slice.3
  190.2 0.0 collective-permute-done
  190.2 0.0 copy-start
  190.2 8.0 %select_bitcast_fusion = bf16[1,768,4096]{2,1,0:T(8,128)(2,1)} fusion(bf16[768,4096]{1,0:T(8,128)(2,1)} %collective-permute-done, pred[]{:T(512)} %bitcast.7, bf16[1,768,4096]{2,1,0:T(8,128)(2,1)} %param.10), kind=kLoop, calls=%fused_computation.1 | loop fusion | flops 3145728 | bytes 18874368 | tf_op jit(solution)/shard_map/broadcast_in_dim | solution.py:519
  198.2 0.0 copy-done
  198.2 0.7 copy.10
  (1 shorter events, 0.0 us)
Async XLA Ops:
  0.6 189.5 %collective-permute-start = (bf16[768,4096]{1,0:T(8,128)(2,1)}, bf16[768,4096]{1,0:T(8,128)(2,1)}, u32[]{:S(2)}, u32[]{:S(2)}) collective-permute-start(bf16[768,4096]{1,0:T(8,128)(2,1)} %bitcast.11), channel_id=1, source_target_pairs={{0,2},{2,0},{4,6},{6,4},{8,10},{10,8},{12,14},{14,12},{16,18},{18,... | collective-permute-start | bytes 18874376 | tf_op jit(solution)/shard_map/ppermute | solution.py:500
  190.2 8.0 %copy-start = (bf16[48,4096]{1,0:T(8,128)(2,1)S(1)}, bf16[48,4096]{1,0:T(8,128)(2,1)}, u32[]{:S(2)}) copy-start(bf16[48,4096]{1,0:T(8,128)(2,1)} %shard_map.77) | copy-start | bytes 1179652

commit v3 on v2

--- a/solution.py
+++ b/solution.py
@@ -16,7 +16,7 @@
 META = 128
 OWN, OTHER = 0, 1
 UP, DOWN = 0, 1
-LAG = 2
+LAG = 4
 OFFSETS = (0, 3, 1, 2)
 BF16 = jnp.bfloat16
 F32 = jnp.float32
@@ -282,23 +282,24 @@
         part = functools.partial
         chunks = 2 * half // chunk
         lag = min(LAG, chunks)
-        actions = [part(select, s, 0), part(select, s, 1)]
+        actions = [(1.5, part(select, s, 0)), (1.5, part(select, s, 1))]
+
+        def add(weight, action):
+            actions.append((weight, action))
+
         if s == 0:
-            actions.append(lambda: [load.wait() for load in loads])
-        actions.append(lambda: [copy.wait_send() for copy in ag_started[s]])
-        actions.append(
-            lambda: [pick_copy(s, grp, h).wait() for grp in (0, 1) for h in (0, 1)]
-        )
-        actions += [part(ffn_up, s, c) for c in range(hidden_width // act_chunk)]
+            add(0, lambda: [load.wait() for load in loads])
+        add(0, lambda: [copy.wait_send() for copy in ag_started[s]])
+        add(0.5, lambda: [pick_copy(s, grp, h).wait() for grp in (0, 1) for h in (0, 1)])
+        for c in range(hidden_width // act_chunk):
+            add(2.0, part(ffn_up, s, c))
         for c in range(chunks + lag):
             if c < chunks:
-                actions.append(part(ffn_down, s, c))
+                add(0.4, part(ffn_down, s, c))
             if c >= lag:
-                actions.append(lambda c=c: back_copy(s, c - lag).wait())
-                actions += [part(partial_sums, s, grp, c - lag) for grp in (0, 1)]
-                for h in (0, 1):
-                    if (c - lag + 1) * chunk == (h + 1) * half:
-                        actions.append(part(run, rs_parts[s][h][0]))
+                add(0.1, lambda c=c: back_copy(s, c - lag).wait())
+                for grp in (0, 1):
+                    add(0.3, part(partial_sums, s, grp, c - lag))
         return actions
 
     rs_started = []
@@ -408,20 +409,18 @@
             action()
 
     def blend(*lists):
-        total = max(len(one) for one in lists)
         merged = []
         for index, one in enumerate(lists):
-            for at, action in enumerate(one):
-                merged.append(((at + 0.5) / len(one), index, at, action))
+            pairs = [item if isinstance(item, tuple) else (1, item) for item in one]
+            total, before = sum(weight for weight, _ in pairs), 0
+            for at, (weight, action) in enumerate(pairs):
+                merged.append(((before + 0.5 * weight) / total, index, at, action))
+                before += weight
         merged.sort(key=lambda item: item[:3])
         return [item[3] for item in merged]
 
     ag = [both(ag_actions, s) for s in range(STEPS)]
-    rs_parts = [[rs_actions(h, s) for h in (0, 1)] for s in range(STEPS)]
-    rs = [
-        [[act_ for pair in zip(pa, pb) for act_ in pair] for pa, pb in zip(*parts)]
-        for parts in rs_parts
-    ]
+    rs = [both(rs_actions, s) for s in range(STEPS)]
     ex = [expert_actions(s) for s in range(STEPS)]
 
     run(ag[0][0])
@@ -430,12 +429,16 @@
     run(ag[0][1])
     run(ag[1][0])
     run(ag[0][2])
-    run(blend(ag[1][1] + ag[2][0], ex[0]))
+    run(blend(ag[1][1], ex[0]))
+    run(ag[2][0])
+    run(rs[0][0])
     run(ag[1][2])
     run(blend(ag[2][1], ex[1], rs[0][1]))
+    run(rs[1][0])
     run(ag[2][2])
     run(rs[0][2])
     run(blend(ex[2], rs[1][1]))
+    run(rs[2][0])
     run(rs[1][2])
     run(rs[2][1])
     run(rs[2][2])
@@ -491,6 +494,55 @@
     )(experts, tok_a, tokens, wgu, wd)
 
 
+PIECES = 6
+
+
+def relocate_kernel(swap_ref, own, other, out, held, in_sem, out_sem):
+    depth = held.shape[0] // PIECES
+    moved = swap_ref[lax.axis_index("ep")] < STEPS
+    parts = [pl.ds(i * depth, depth) for i in range(PIECES)]
+
+    def load(source, i):
+        return pltpu.make_async_copy(
+            source.at[parts[i], :], held.at[parts[i], :], in_sem.at[i]
+        )
+
+    for source, wanted in ((other, moved), (own, jnp.logical_not(moved))):
+
+        @pl.when(wanted)
+        def _():
+            for i in range(PIECES):
+                load(source, i).start()
+
+    stores = []
+    for i in range(PIECES):
+        load(own, i).wait()
+        stores.append(
+            pltpu.make_async_copy(held.at[parts[i], :], out.at[parts[i], :], out_sem.at[i])
+        )
+        stores[-1].start()
+    for store in stores:
+        store.wait()
+
+
+def relocate(swap_step, own, other):
+    return pl.pallas_call(
+        relocate_kernel,
+        out_shape=jax.ShapeDtypeStruct(own.shape, own.dtype),
+        in_specs=[pl.BlockSpec(memory_space=pltpu.SMEM)]
+        + [pl.BlockSpec(memory_space=pl.ANY)] * 2,
+        out_specs=pl.BlockSpec(memory_space=pl.ANY),
+        scratch_shapes=[
+            pltpu.VMEM(own.shape, own.dtype),
+            pltpu.SemaphoreType.DMA((PIECES,)),
+            pltpu.SemaphoreType.DMA((PIECES,)),
+        ],
+        cost_estimate=pl.CostEstimate(
+            flops=0, bytes_accessed=4 * own.size, transcendentals=0
+        ),
+    )(swap_step, own, other)
+
+
 def on_device(hidden, expert_ids, gate_logits, w_gate_up, w_down, swap_step):
     devices = lax.axis_size("ep")
     my_index = lax.axis_index("ep")
@@ -515,7 +567,7 @@
         w_gate_up[0],
         w_down[0],
     )
-    relocated = jnp.where(swap_step[my_index] < num_steps, other_down, w_down[0])
+    relocated = relocate(swap_step, w_down[0], other_down)
     return (mixed.reshape(hidden.shape), relocated[None])
 
 

time: 199 us -> 175 us (0.88)
  Pallas kernels: 184 us -> 170 us
  other arithmetic: 10.8 us -> 2.75 us
    pallas_call x1, Pallas kernels: 184 us -> 163 us  [moe(): pl.pallas_call(moe_kernel, out_shape=jax.ShapeDtypeStruct((rows, 2 * half...]
    broadcast_in_dim x1 -> x0, other arithmetic: 8.01 us -> none  [on_device(): return (mixed.reshape(hidden.shape), relocated[None])]
    pallas_call x0 -> x1, Pallas kernels: none -> 6.27 us  [relocate(): pl.pallas_call(relocate_kernel, out_shape=jax.ShapeDtypeStruct(own.shape,...]
  transfers between devices with their start and end apart: 1 -> 1, of which waited for: 0 -> 0; matrix products, arithmetic and copies ran while one was open for 3% -> 2% of each run, Pallas kernels for 92% -> 93%
where the time goes in v3:
time: 175 us
  Pallas kernels  170 us (97%)
  other arithmetic  2.75 us (2%)
  local copies, waits for them, and re-layouts  1.78 us (1%)
    pallas_call x1, Pallas kernels, moe(): pl.pallas_call(moe_kernel, out_shape=jax.ShapeDtypeStruct((rows, 2 * half...  163 us
    pallas_call x1, Pallas kernels, relocate(): pl.pallas_call(relocate_kernel, out_shape=jax.ShapeDtypeStruct(own.shape,...  6.27 us
  transfers between devices with their start and end apart: 1, of which 0 were waited for; matrix products, arithmetic and copies ran while one was open for 2% of the time, Pallas kernels for 93%

profile of v3, /device:TPU:0, one launch (start us, length us, event | category | flops | bytes accessed | tf_op | source)
XLA Modules:
  0.0 174.9 jit_solution(10410874570848033638)
XLA Ops:
  0.6 0.1 collective-permute-start
  0.7 0.7 convert_convert_fusion
  1.4 0.7 reduce-precision_convert_fusion
  2.2 0.1 copy.8
  2.3 0.9 slice.4
  3.2 0.6 add_convert_fusion.expert_ref
  3.8 0.7 fusion.3.tok_a
  4.5 163.3 %shard_map.77 = bf16[48,4096]{1,0:T(8,128)(2,1)} custom-call(f32[2]{0:T(128)} %add_convert_fusion.expert_ref, bf16[48,2176]{1,0:T(8,128)(2,1)} %fusion.3.tok_a, bf16[48,4096]{1,0:T(8,128)(2,1)} %bitcast.15, bf16[4096,1536]{1,0:T(8,128)(2,1)} %bitcast.11, bf16[768,4096]{1,0:T(8,128)(2,1)} %bitcast.9), custom_call_target="tpu_custom_call" | custom-call | tf_op jit(solution)/shard_map/pallas_call | solution.py:457
  167.8 0.0 copy-start
  167.8 0.0 collective-permute-done.other
  167.8 6.3 %shard_map.78 = bf16[768,4096]{1,0:T(8,128)(2,1)} custom-call(s32[64]{0:T(128)} %swap_ref.1, bf16[768,4096]{1,0:T(8,128)(2,1)} %bitcast.10, bf16[768,4096]{1,0:T(8,128)(2,1)} %collective-permute-done.other), custom_call_target="tpu_custom_call" | custom-call | bytes 12582912 | tf_op jit(solution)/shard_map/pallas_call | solution.py:529
  174.1 0.0 copy-done
  174.1 0.7 copy.10
  (1 shorter events, 0.0 us)
Async XLA Ops:
  0.6 167.2 %collective-permute-start = (bf16[768,4096]{1,0:T(8,128)(2,1)}, bf16[768,4096]{1,0:T(8,128)(2,1)}, u32[]{:S(2)}, u32[]{:S(2)}) collective-permute-start(bf16[768,4096]{1,0:T(8,128)(2,1)} %bitcast.8), channel_id=1, source_target_pairs={{0,2},{2,0},{4,6},{6,4},{8,10},{10,8},{12,14},{14,12},{16,18},{18,... | collective-permute-start | bytes 18874376 | tf_op jit(solution)/shard_map/ppermute | solution.py:552
  167.8 6.3 %copy-start = (bf16[48,4096]{1,0:T(8,128)(2,1)S(1)}, bf16[48,4096]{1,0:T(8,128)(2,1)}, u32[]{:S(2)}) copy-start(bf16[48,4096]{1,0:T(8,128)(2,1)} %shard_map.77) | copy-start | bytes 1179652
